TPU v7x, 128 devices: a whole 4x4x4 slice. The times are simulated.
128 devices in a mesh: mem: 8 (over x, core), tile: 16 (over z, y).
Axes of the slice: x: 4, y: 4, z: 4, core: 2. Of those that a mesh axis runs over, the one named last changes fastest.
Arguments:
- members: bfloat16 [16, 137, 8192], P('mem', None, 'tile'), may hold values from -18 to 18
- vertical: bfloat16 [137, 137], replicated, may hold values from 0 to 1, as said below
- jacobian: bfloat16 [2048, 231, 137], P('tile'), may hold values from -0.5 to 0.5
- sketch_bits: int32 [3, 2048, 231], P(None, 'tile'), may hold values from 0 to 1
- test_bits: int32 [3, 2048, 231], P(None, 'tile'), may hold values from 0 to 1
- obs_column: int32 [2048], P('tile'), may hold values from 0 to 8191, as said below
- obs_slot: int32 [2048], P('tile'), may hold values from 0 to 31, as said below
Outputs:
- image_q: float32 [3, 2048, 231], P(None, 'tile')
- image_w: float32 [3, 2048, 231], P(None, 'tile')
- trace_mean: float32 [], replicated
- sketch_rayleigh: float32 [], replicated
Inputs may be any that keep to these rules, and one draw needn't show every extreme that they name: The observations of owner d are rows d * 128 to (d + 1) * 128 - 1; an observation's column lies in tile obs_column // 512. `obs_slot`: among one owner's observations whose columns lie in the same tile the slots are distinct, so at most 32 of them lie in one tile; every owner has exactly 32 observations in some tile. A vertical correlation matrix: symmetric, positive semidefinite, with ones on the diagonal.
All inputs are finite; a program needn't handle non-finite values.
Results may differ from a plain program's by a relative error of at most 0.0053.
Values may be sent and summed in bfloat16 or wider, within the bound.
No kernel may reach another device: no remote copies, remote signals or barrier semaphores. Data moves between devices by JAX's collectives and lax.ppermute only.
A program may use at most 128 MiB of HBM per device.

v0:
```python
import jax
import jax.numpy as jnp
from jax import lax
from jax.sharding import Mesh
from jax.sharding import PartitionSpec as P

CB = 32
K = 3
STEPS = 6
TILE = ("tile_0", "tile_1")
diffusion_rate = 0.2
highest = lax.Precision.HIGHEST


def with_halo(block, sides, width):
    for axis, dim in sides:
        count = lax.axis_size(axis)
        forward = [(i, i + 1) for i in range(count - 1)]
        forward.append((count - 1, 0))
        backward = [(target, source) for source, target in forward]
        low = lax.ppermute(
            lax.slice_in_dim(block, block.shape[dim] - width, None, axis=dim), axis, forward
        )
        high = lax.ppermute(lax.slice_in_dim(block, 0, width, axis=dim), axis, backward)
        block = jnp.concatenate([low, block, high], axis=dim)
    return block


def gather_turned(arrays, axis, dims):
    turned = [jnp.moveaxis(a, dim, 0) for a, dim in zip(arrays, dims)]
    widths = [t[0].size for t in turned]
    both = jnp.concatenate([t.reshape(-1, w) for t, w in zip(turned, widths)], axis=1)
    whole = lax.all_gather(both, axis, axis=0, tiled=True)
    pieces = jnp.split(whole, [sum(widths[:k]) for k in range(1, len(widths))], axis=1)
    return tuple(
        (
            jnp.moveaxis(b.reshape(-1, *t.shape[1:]), 0, dim)
            for b, t, dim in zip(pieces, turned, dims)
        )
    )


def split_up(value, dim, peers):
    before, after = (value.shape[:dim], value.shape[dim + 1 :])
    return jnp.moveaxis(value.reshape(*before, peers, -1, *after), dim, 0)


def sum_at_owner(value, axis, dim):
    pieces = split_up(value, dim, lax.axis_size(axis))
    arrived = lax.all_to_all(pieces, axis, split_axis=0, concat_axis=0, tiled=True)
    return arrived.sum(axis=0)


def from_everyone(value, axis):
    peers = lax.axis_size(axis)
    return lax.all_to_all(
        jnp.broadcast_to(value[None], (peers, *value.shape)), axis, 0, 0, tiled=True
    )


def joined_along(pieces, dim):
    lengths = list(pieces.shape[1:])
    lengths[dim] *= pieces.shape[0]
    return jnp.moveaxis(pieces, 0, dim).reshape(lengths)


def collect_2(value, axis, dim):
    pieces = from_everyone(value, axis)
    return joined_along(pieces, dim)


def by_axis(value, axes):
    for axis in axes:
        value = lax.psum(value, axis)
    return value


def relax(extended):
    length = extended.shape[-1] - 2 * CB
    center = extended[..., CB : CB + length]
    places = jnp.arange(length) % CB
    west_ok = (places > 0).astype(jnp.float32)
    east_ok = (places < CB - 1).astype(jnp.float32)
    north = extended[..., :length]
    south = extended[..., 2 * CB :]
    west = extended[..., CB - 1 : CB - 1 + length]
    east = extended[..., CB + 1 : CB + 1 + length]
    return center + diffusion_rate * (
        north - center + (south - center) + west_ok * (west - center) + east_ok * (east - center)
    )


def diffuse(state):
    extended = with_halo(state, ((TILE, 2),), STEPS * CB)
    for _ in range(STEPS):
        extended = relax(extended)
    return extended


def on_device(members, vertical, jacobian, sketch_bits, test_bits, obs_column, obs_slot):
    tile_count = lax.axis_size(TILE)
    my_tile = lax.axis_index(TILE)
    obs_local = obs_column.shape[0]
    levels = members.shape[1]
    cell_count = members.shape[2]
    channels = jacobian.shape[1]
    capacity = obs_local // 4
    slot_count = tile_count * capacity
    ensemble = members.shape[0] * lax.axis_size("mem")
    count = float(obs_local * tile_count * channels)
    all_columns, all_slots = gather_turned((obs_column, obs_slot), TILE, (0, 0))
    owners = jnp.arange(tile_count * obs_local, dtype=jnp.int32) // obs_local
    target = jnp.where(
        all_columns // cell_count == my_tile, owners * capacity + all_slots, slot_count
    )
    cell_table = (
        jnp.zeros((slot_count,), jnp.int32).at[target].set(all_columns % cell_count, mode="drop")
    )
    occupied = jnp.zeros((slot_count,), jnp.bool_).at[target].set(True, mode="drop")
    spread = ((cell_table[:, None] == jnp.arange(cell_count)[None, :]) & occupied[:, None]).astype(
        jnp.bfloat16
    )
    my_positions = obs_column // cell_count * capacity + obs_slot
    collect = (my_positions[:, None] == jnp.arange(slot_count)[None, :]).astype(jnp.bfloat16)

    def apply_operator(vectors):
        probes = vectors.shape[0]
        rows = probes * levels
        adjoint = jnp.einsum(
            "ocl,poc->plo",
            jacobian,
            vectors.astype(jnp.bfloat16),
            preferred_element_type=jnp.float32,
        ).astype(jnp.bfloat16)
        outgoing = jnp.dot(
            adjoint.reshape(rows, obs_local), collect, preferred_element_type=jnp.float32
        ).astype(jnp.bfloat16)
        arrived = lax.all_to_all(outgoing, TILE, split_axis=1, concat_axis=1, tiled=True)
        field_sum = jnp.dot(arrived, spread, preferred_element_type=jnp.float32).reshape(
            probes, levels, cell_count
        )

        def member_step(number, carry):
            member = lax.dynamic_index_in_dim(members, number, 0, keepdims=False).astype(
                jnp.float32
            )
            product = (member[None] * field_sum).astype(jnp.bfloat16)
            mixed = jnp.einsum("kl,plc->pkc", vertical, product, preferred_element_type=jnp.float32)
            return carry + member[None] * diffuse(mixed)

        partial_sum = lax.fori_loop(
            0, members.shape[0], member_step, jnp.zeros((probes, levels, cell_count), jnp.float32)
        )
        partial_cols = jnp.take(partial_sum.reshape(rows, cell_count), cell_table, axis=1).reshape(
            rows, tile_count, capacity
        )
        picked = sum_at_owner(partial_cols, "mem", 2) / (ensemble - 1)
        outbound = picked.astype(jnp.bfloat16)
        returned = lax.all_to_all(outbound, TILE, split_axis=1, concat_axis=1, tiled=True)
        returned = collect_2(returned, "mem", 2)
        returned = returned.reshape(rows, slot_count)
        profile = jnp.dot(returned, collect.T, preferred_element_type=jnp.float32).astype(
            jnp.bfloat16
        )
        profile = profile.reshape(probes, levels, obs_local)
        return jnp.einsum("ocl,plo->poc", jacobian, profile, preferred_element_type=jnp.float32)

    sketch = (2 * sketch_bits - 1).astype(jnp.float32)
    test = (2 * test_bits - 1).astype(jnp.float32)
    sketch_image = apply_operator(sketch)
    products = by_axis(
        jnp.einsum("ioc,joc->ij", sketch_image, sketch_image, precision=highest), TILE
    )
    lower = jnp.linalg.cholesky(products)
    inverse_lower = lax.linalg.triangular_solve(
        lower, jnp.eye(K, dtype=jnp.float32), left_side=True, lower=True
    )
    basis = jnp.sqrt(count) * jnp.einsum(
        "ji,ioc->joc", inverse_lower, sketch_image, precision=highest
    )
    intersection = by_axis(jnp.einsum("ioc,joc->ij", basis, test, precision=highest), TILE) / count
    remainder = test - jnp.einsum("ij,ioc->joc", intersection, basis, precision=highest)
    images = apply_operator(jnp.concatenate([basis, remainder], axis=0))
    image_q = images[:K]
    image_w = images[K:]
    trace_q, trace_w = (
        by_axis(jnp.sum(basis * image_q), TILE),
        by_axis(jnp.sum(remainder * image_w), TILE),
    )
    trace_mean = trace_q / (count * count) + trace_w / (K * count)
    sketch_rayleigh = trace_q / (K * count)
    return (image_q, image_w, trace_mean, sketch_rayleigh)


def solution(mesh):
    finer = Mesh(mesh.devices.reshape(mesh.shape["mem"], 4, 4), ("mem", "tile_0", "tile_1"))
    return jax.shard_map(
        on_device,
        mesh=finer,
        in_specs=(
            P("mem", None, TILE),
            P(),
            P(TILE, None, None),
            P(None, TILE, None),
            P(None, TILE, None),
            P(TILE),
            P(TILE),
        ),
        out_specs=(P(None, TILE, None), P(None, TILE, None), P(), P()),
        check_vma=False,
    )
```

profile of v0, /device:TPU:0, one launch (start us, length us, event | category | flops | bytes accessed | tf_op | source)
XLA Modules:
  0.0 431.1 jit_solution(6855449706677383312)
XLA Ops:
  0.6 13.3 %copy.96 = bf16[128,231,137]{1,2,0:T(8,128)(2,1)} copy(bf16[128,231,137]{0,1,2:T(8,128)(2,1)} %param.13) | data formatting | bytes 16203264 | tf_op args[2]
  14.2 6.2 %fusion.179 = bf16[3,137,128]{1,0,2:T(4,128)(2,1)S(1)} fusion(bf16[3,128,231]{2,0,1:T(4,128)(2,1)S(1)} %copy.95, bf16[128,231,137]{1,2,0:T(8,128)(2,1)} %copy.96), kind=kOutput, calls=%fused_computation.270 | convolution fusion | flops 24357504 | bytes 8384256 | tf_op jit(solution)/shard_map/ocl,poc->plo/dot_general | solution.py:129
  22.1 8.2 %all-to-all-start = ((bf16[411,16,32]{0,2,1:T(8,128)(2,1)}), bf16[411,16,32]{0,2,1:T(8,128)(2,1)S(1)}, u32[]{:S(2)}, u32[]{:S(2)}) async-start(bf16[411,16,32]{0,2,1:T(8,128)(2,1)} %bitcast.5), calls=%async_computation | async-start | bytes 1048576 | tf_op jit(solution)/shard_map/all_to_all | solution.py:138
  30.2 25.7 %all_gather.3 = s32[2048,2]{0,1:T(2,128)S(1)} all-gather(s32[128,2]{0,1:T(2,128)S(1)} %pad_add_fusion), channel_id=1, replica_groups=mesh['mem'=8,'tile_0'=4,'tile_1'=4] {'tile_0','tile_1'}, dimensions={0}, use_global_device_ids=true | all-gather | bytes 17408 | tf_op jit(solution)/shard_map/all_gather | solution.py:33
  56.1 8.0 %scatter_custom_fusion = s32[512]{0:T(512)S(1)} fusion(s32[2048]{0:T(1024)S(1)} %bitcast.110, s32[2048]{0:T(1024)S(1)} %add_select_fusion.12, s32[]{:T(128)} %constant.386.clone.1), kind=kCustom, calls=%fused_computation.340 | custom fusion | bytes 2052 | tf_op jit(solution)/shard_map/scatter | solution.py:117
  64.3 9.1 %scatter_custom_fusion.1 = pred[512]{0:T(512)(128)(4,1)S(1)} fusion(s32[2048]{0:T(1024)S(1)} %bitcast.111, pred[2048]{0:T(1024)(128)(4,1)S(1)} %broadcast.1456, pred[]{:T(512)} %constant.400.clone.1), kind=kCustom, calls=%fused_computation.342 | custom fusion | bytes 513 | tf_op jit(solution)/shard_map/scatter | solution.py:119
  75.1 1.9 fusion.183
  77.0 49.0 %while.32 = (s32[]{:T(128)}, f32[3,137,512]{2,1,0:T(8,128)S(1)}, bf16[2,137,512]{2,1,0:T(8,128)(2,1)S(1)}, f32[3,137,512]{2,1,0:T(8,128)S(1)}, bf16[137,137]{1,0:T(8,128)(2,1)S(1)}, /*index=5*/s32[]{:T(128)}, s32[]{:T(128)}) while((s32[]{:T(128)}, f32[3,137,512]{2,1,0:T(8,128)S(1)}, bf16[2,137,512]{2,1,0:T(8,128)(2,1)S(1)}, ...), condition=%wide.region_3.4_spmd.clone, body=%wide.region_2.3_spmd.clone.sunk | while | flops 77786176 | bytes 52359552 | solution.py:151
  78.9 2.1 collective-permute-start
  81.0 6.5 %collective-permute-done = f32[3,137,192]{2,1,0:T(8,128)} collective-permute-done((f32[3,137,192]{2,1,0:T(8,128)}, f32[3,137,192]{2,1,0:T(8,128)}, u32[]{:S(2)}, u32[]{:S(2)}) %collective-permute-start) | collective-permute-done | bytes 315680 | tf_op jit(solution)/shard_map/while/body/eval_jaxpr/ppermute | solution.py:24
  87.5 5.2 %collective-permute-done.1 = f32[3,137,192]{2,1,0:T(8,128)} collective-permute-done((f32[3,137,192]{2,1,0:T(8,128)S(1)}, f32[3,137,192]{2,1,0:T(8,128)}, u32[]{:S(2)}, u32[]{:S(2)}) %collective-permute-start.1) | collective-permute-done | bytes 315680 | tf_op jit(solution)/shard_map/while/body/eval_jaxpr/ppermute | solution.py:21
  92.7 1.6 pad_maximum_fusion.5
  94.3 1.7 fusion.266
  104.5 1.8 collective-permute-start.1
  106.4 6.5 %collective-permute-done = f32[3,137,192]{2,1,0:T(8,128)} collective-permute-done((f32[3,137,192]{2,1,0:T(8,128)}, f32[3,137,192]{2,1,0:T(8,128)}, u32[]{:S(2)}, u32[]{:S(2)}) %collective-permute-start) | collective-permute-done | bytes 315680 | tf_op jit(solution)/shard_map/while/body/eval_jaxpr/ppermute | solution.py:24
  112.9 3.3 collective-permute-done.1
  117.9 1.7 fusion.266
  127.1 1.6 gather_fusion
  129.5 20.5 %all_to_all.48 = f32[8,411,16,4]{1,3,2,0:T(4,128)S(1)} all-to-all(f32[8,411,16,4]{1,3,2,0:T(4,128)S(1)} %copy.102), channel_id=1, replica_groups=mesh['mem'=8,'tile_0'=4,'tile_1'=4] {'mem'}, dimensions={0} | all-to-all | bytes 1683456 | tf_op jit(solution)/shard_map/all_to_all | solution.py:50
  150.3 10.2 %all_to_all.49 = bf16[411,16,4]{0,2,1:T(4,128)(2,1)S(1)} all-to-all(bf16[411,16,4]{0,2,1:T(4,128)(2,1)S(1)} %multiply_convert_fusion.5), channel_id=1, replica_groups=mesh['mem'=8,'tile_0'=4,'tile_1'=4] {'tile_0','tile_1'}, dimensions={1} | all-to-all | bytes 105216 | tf_op jit(solution)/shard_map/all_to_all | solution.py:159
  160.6 12.8 %all_to_all.50 = bf16[8,411,16,4]{1,3,2,0:T(4,128)(2,1)S(1)} all-to-all(bf16[8,411,16,4]{1,3,2,0:T(4,128)(2,1)S(1)} %broadcast_in_dim.146), channel_id=1, replica_groups=mesh['mem'=8,'tile_0'=4,'tile_1'=4] {'mem'}, dimensions={0} | all-to-all | bytes 841728 | tf_op jit(solution)/shard_map/all_to_all | solution.py:56
  174.5 5.0 %convolution_bitcast_fusion.2 = f32[3,128,231]{2,0,1:T(4,128)S(1)} fusion(bf16[3,137,128]{1,0,2:T(4,128)(2,1)S(1)} %copy.104, bf16[128,231,137]{1,2,0:T(8,128)(2,1)} %copy.96), kind=kOutput, calls=%fused_computation.267 | convolution fusion | flops 24304896 | bytes 8561664 | tf_op jit(solution)/shard_map/ocl,plo->poc/dot_general | solution.py:166
  179.6 2.3 convolution_bitcast_fusion.5
  182.0 8.8 %psum.56 = f32[3,3]{0,1:T(4,128)S(1)} all-reduce(f32[3,3]{0,1:T(4,128)S(1)} %convolution_bitcast_fusion.5), channel_id=1, replica_groups=mesh['mem'=8,'tile_0'=4,'tile_1'=4] {'tile_0'}, use_global_device_ids=true, to_apply=%region_5.6 | all-reduce | flops 9 | bytes 72 | tf_op jit(solution)/shard_map/psum | solution.py:74
  191.1 8.9 %psum.57 = f32[3,3]{0,1:T(4,128)S(1)} all-reduce(f32[3,3]{0,1:T(4,128)S(1)} %psum.56), channel_id=1, replica_groups=mesh['mem'=8,'tile_0'=4,'tile_1'=4] {'tile_1'}, use_global_device_ids=true, to_apply=%region_6.7 | all-reduce | flops 9 | bytes 72 | tf_op jit(solution)/shard_map/psum | solution.py:74
  203.2 2.2 convolution_bitcast_fusion.3
  205.4 8.6 %psum.58 = f32[3,3]{1,0:T(4,128)S(1)} all-reduce(f32[3,3]{1,0:T(4,128)S(1)} %convolution_bitcast_fusion.3), channel_id=1, replica_groups=mesh['mem'=8,'tile_0'=4,'tile_1'=4] {'tile_0'}, use_global_device_ids=true, to_apply=%region_9.10 | all-reduce | flops 9 | bytes 72 | tf_op jit(solution)/shard_map/psum | solution.py:74
  214.0 8.6 %psum.59 = f32[3,3]{1,0:T(4,128)S(1)} all-reduce(f32[3,3]{1,0:T(4,128)S(1)} %psum.58), channel_id=1, replica_groups=mesh['mem'=8,'tile_0'=4,'tile_1'=4] {'tile_1'}, use_global_device_ids=true, to_apply=%region_10.11 | all-reduce | flops 9 | bytes 72 | tf_op jit(solution)/shard_map/psum | solution.py:74
  224.3 6.2 %fusion.178 = bf16[6,137,128]{1,0,2:T(8,128)(2,1)S(1)} fusion(bf16[6,128,231]{2,0,1:T(8,128)(2,1)S(1)} %copy.116, bf16[128,231,137]{1,2,0:T(8,128)(2,1)} %copy.96), kind=kOutput, calls=%fused_computation.266 | convolution fusion | flops 48715008 | bytes 8666880 | tf_op jit(solution)/shard_map/ocl,poc->plo/dot_general | solution.py:129
  232.7 3.6 all-to-all-start.4
  236.3 12.4 %all-to-all-done.4 = bf16[822,16,32]{0,2,1:T(8,128)(2,1)S(1)} async-done(((bf16[822,16,32]{0,2,1:T(8,128)(2,1)}), bf16[822,16,32]{0,2,1:T(8,128)(2,1)S(1)}, u32[]{:S(2)}, u32[]{:S(2)}) %all-to-all-start.4) | async-done | bytes 841760 | tf_op jit(solution)/shard_map/all_to_all | solution.py:138
  248.7 3.1 dot_general.78
  251.8 3.8 fusion.176
  255.6 79.9 %while.33 = (s32[]{:T(128)}, f32[6,137,512]{2,1,0:T(8,128)}, bf16[2,137,512]{2,1,0:T(8,128)(2,1)S(1)}, f32[6,137,512]{2,1,0:T(8,128)}, bf16[137,137]{1,0:T(8,128)(2,1)S(1)}, /*index=5*/s32[]{:T(128)}, s32[]{:T(128)}) while((s32[]{:T(128)}, f32[6,137,512]{2,1,0:T(8,128)}, bf16[2,137,512]{2,1,0:T(8,128)(2,1)S(1)}, ...), condition=%wide.region_12.13_spmd.clone, body=%wide.region_11.12_spmd.clone.sunk | while | flops 155461888 | bytes 112613240 | solution.py:151
  255.8 2.0 convolution_bitcast_fusion.9
  261.1 11.3 %collective-permute-done.2 = f32[6,137,192]{2,1,0:T(8,128)} collective-permute-done((f32[6,137,192]{2,1,0:T(8,128)}, f32[6,137,192]{2,1,0:T(8,128)}, u32[]{:S(2)}, u32[]{:S(2)}) %collective-permute-start.2) | collective-permute-done | bytes 631328 | tf_op jit(solution)/shard_map/while/body/eval_jaxpr/ppermute | solution.py:24
  272.4 4.3 collective-permute-done.3
  276.7 2.3 pad_maximum_fusion.6
  279.0 3.4 fusion.280
  282.4 2.8 fusion.282
  285.2 2.8 fusion.284
  288.0 2.3 fusion.286
  290.4 2.3 fusion.288
  292.7 2.1 fusion.290
  296.1 2.0 convolution_bitcast_fusion.9
  299.5 1.8 collective-permute-start.3
  301.4 11.3 %collective-permute-done.2 = f32[6,137,192]{2,1,0:T(8,128)} collective-permute-done((f32[6,137,192]{2,1,0:T(8,128)}, f32[6,137,192]{2,1,0:T(8,128)}, u32[]{:S(2)}, u32[]{:S(2)}) %collective-permute-start.2) | collective-permute-done | bytes 631328 | tf_op jit(solution)/shard_map/while/body/eval_jaxpr/ppermute | solution.py:24
  312.7 3.3 collective-permute-done.3
  316.0 2.3 pad_maximum_fusion.6
  318.3 3.4 fusion.280
  321.7 2.8 fusion.282
  324.5 2.8 fusion.284
  327.3 2.3 fusion.286
  329.6 2.3 fusion.288
  332.0 2.1 fusion.290
  335.5 1.8 reshape.300
  338.1 2.6 gather_fusion.1
  340.7 1.8 gather.15
  343.3 26.8 %all_to_all.51 = f32[8,822,16,4]{1,3,2,0:T(4,128)S(1)} all-to-all(f32[8,822,16,4]{1,3,2,0:T(4,128)S(1)} %copy.123), channel_id=1, replica_groups=mesh['mem'=8,'tile_0'=4,'tile_1'=4] {'mem'}, dimensions={0} | all-to-all | bytes 3366912 | tf_op jit(solution)/shard_map/all_to_all | solution.py:50
  370.6 10.5 %all_to_all.52 = bf16[822,16,4]{0,2,1:T(4,128)(2,1)S(1)} all-to-all(bf16[822,16,4]{0,2,1:T(4,128)(2,1)S(1)} %multiply_convert_fusion.4), channel_id=1, replica_groups=mesh['mem'=8,'tile_0'=4,'tile_1'=4] {'tile_0','tile_1'}, dimensions={1} | all-to-all | bytes 210432 | tf_op jit(solution)/shard_map/all_to_all | solution.py:159
  381.4 17.0 %all_to_all.53 = bf16[8,822,16,4]{1,3,2,0:T(4,128)(2,1)S(1)} all-to-all(bf16[8,822,16,4]{1,3,2,0:T(4,128)(2,1)S(1)} %broadcast_in_dim.148), channel_id=1, replica_groups=mesh['mem'=8,'tile_0'=4,'tile_1'=4] {'mem'}, dimensions={0} | all-to-all | bytes 1683456 | tf_op jit(solution)/shard_map/all_to_all | solution.py:56
  400.1 5.0 %fusion.218 = f32[128,6,231]{2,1,0:T(8,128)S(1)} fusion(bf16[6,137,128]{1,0,2:T(8,128)(2,1)S(1)} %copy.125, bf16[128,231,137]{1,2,0:T(8,128)(2,1)} %copy.96), kind=kOutput, calls=%fused_computation.351 | convolution fusion | flops 48609792 | bytes 9021696 | tf_op jit(solution)/shard_map/ocl,plo->poc/dot_general | solution.py:166
  407.9 9.2 %all-reduce.1 = (f32[]{:T(128)}, f32[]{:T(128)}) all-reduce(f32[]{:T(128)} %get-tuple-element.418, f32[]{:T(128)} %get-tuple-element.384), channel_id=1, replica_groups=mesh['mem'=8,'tile_0'=4,'tile_1'=4] {'tile_0'}, use_global_device_ids=true, to_apply=%region_15.16 | all-reduce | flops 2 | bytes 16 | tf_op jit(solution)/shard_map/psum | solution.py:74
  417.1 9.6 %all-reduce = (f32[]{:T(128)}, f32[]{:T(128)}) all-reduce(f32[]{:T(128)} %get-tuple-element.382, f32[]{:T(128)} %get-tuple-element.383), channel_id=1, replica_groups=mesh['mem'=8,'tile_0'=4,'tile_1'=4] {'tile_1'}, use_global_device_ids=true, to_apply=%region_16.17 | all-reduce | flops 2 | bytes 16 | tf_op jit(solution)/shard_map/psum | solution.py:74
  (168 shorter events, 46.6 us)
Async XLA Ops:
  0.6 13.3 %copy-start.13 = (s32[3,128,231]{1,2,0:T(8,128)S(1)}, s32[3,128,231]{1,2,0:T(8,128)}, u32[]{:S(2)}) copy-start(s32[3,128,231]{1,2,0:T(8,128)} %param.14) | copy-start | bytes 1064452
  14.2 6.4 %copy-start.21 = (s32[128]{0:T(128)S(1)}, s32[128]{0:T(128)}, u32[]{:S(2)}) copy-start(s32[128]{0:T(128)} %param.17) | copy-start | bytes 1540
  14.2 6.4 %copy-start.22 = (s32[128]{0:T(128)S(1)}, s32[128]{0:T(128)}, u32[]{:S(2)}) copy-start(s32[128]{0:T(128)} %param.16) | copy-start | bytes 1540
  20.4 43.7 %copy-start.14 = (bf16[2,137,512]{2,0,1:T(2,128)(2,1)S(1)}, bf16[2,137,512]{2,0,1:T(2,128)(2,1)}, u32[]{:S(2)}) copy-start(bf16[2,137,512]{2,0,1:T(2,128)(2,1)} %param.11) | copy-start | bytes 841732
  20.7 210.2 %copy-start.19 = (s32[128]{0:T(128)}, s32[128]{0:T(128)S(1)}, u32[]{:S(2)}) copy-start(s32[128]{0:T(128)S(1)} %multiply_add_fusion) | copy-start | bytes 1540
  22.1 51.5 %all-to-all-start = ((bf16[411,16,32]{0,2,1:T(8,128)(2,1)}), bf16[411,16,32]{0,2,1:T(8,128)(2,1)S(1)}, u32[]{:S(2)}, u32[]{:S(2)}) async-start(bf16[411,16,32]{0,2,1:T(8,128)(2,1)} %bitcast.5), calls=%async_computation | async-start | bytes 1048576 | tf_op jit(solution)/shard_map/all_to_all | solution.py:138
  64.3 64.8 %copy-start.15 = (pred[16,8,4]{2,1,0:T(8,128)(4,1)}, pred[16,8,4]{2,1,0:T(8,128)(4,1)S(1)}, u32[]{:S(2)}) copy-start(pred[16,8,4]{2,1,0:T(8,128)(4,1)S(1)} %broadcast_in_dim.137) | copy-start | bytes 1540
  73.5 53.6 %copy-start.17 = (s32[1024]{0:T(1024)}, s32[1024]{0:T(1024)S(1)}, u32[]{:S(2)}) copy-start(s32[1024]{0:T(1024)S(1)} %pad_clamp_fusion) | copy-start | bytes 12292
  73.5 3.5 copy-start.8
  77.0 0.7 copy-start.2
  78.9 8.6 %collective-permute-start = (f32[3,137,192]{2,1,0:T(8,128)}, f32[3,137,192]{2,1,0:T(8,128)}, u32[]{:S(2)}, u32[]{:S(2)}) collective-permute-start(f32[3,137,192]{2,1,0:T(8,128)} %get-tuple-element.507), channel_id=1, source_target_pairs={{1,0},{2,1},{3,2},{4,3},{5,4},{6,5},{7,6},{8,7},{9,8},{10,9},{11,1... | collective-permute-start | bytes 946952 | tf_op jit(solution)/shard_map/while/body/eval_jaxpr/ppermute | solution.py:24
  81.0 11.7 %collective-permute-start.1 = (f32[3,137,192]{2,1,0:T(8,128)S(1)}, f32[3,137,192]{2,1,0:T(8,128)}, u32[]{:S(2)}, u32[]{:S(2)}) collective-permute-start(f32[3,137,192]{2,1,0:T(8,128)S(1)} %get-tuple-element.508), channel_id=1, source_target_pairs={{0,1},{1,2},{2,3},{3,4},{4,5},{5,6},{6,7},{7,8},{8,9},{9,10},{10,1... | collective-permute-start | bytes 946952 | tf_op jit(solution)/shard_map/while/body/eval_jaxpr/ppermute | solution.py:21
  101.3 1.1 copy-start.3
  102.4 0.7 copy-start.2
  104.3 8.6 %collective-permute-start = (f32[3,137,192]{2,1,0:T(8,128)}, f32[3,137,192]{2,1,0:T(8,128)}, u32[]{:S(2)}, u32[]{:S(2)}) collective-permute-start(f32[3,137,192]{2,1,0:T(8,128)} %get-tuple-element.507), channel_id=1, source_target_pairs={{1,0},{2,1},{3,2},{4,3},{5,4},{6,5},{7,6},{8,7},{9,8},{10,9},{11,1... | collective-permute-start | bytes 946952 | tf_op jit(solution)/shard_map/while/body/eval_jaxpr/ppermute | solution.py:24
  104.5 11.7 %collective-permute-start.1 = (f32[3,137,192]{2,1,0:T(8,128)S(1)}, f32[3,137,192]{2,1,0:T(8,128)}, u32[]{:S(2)}, u32[]{:S(2)}) collective-permute-start(f32[3,137,192]{2,1,0:T(8,128)S(1)} %get-tuple-element.508), channel_id=1, source_target_pairs={{0,1},{1,2},{2,3},{3,4},{4,5},{5,6},{6,7},{7,8},{8,9},{9,10},{10,1... | collective-permute-start | bytes 946952 | tf_op jit(solution)/shard_map/while/body/eval_jaxpr/ppermute | solution.py:21
  124.8 1.1 copy-start.3
  125.9 0.7 copy-start.4
  174.5 7.4 %copy-start.11 = (s32[3,128,231]{1,2,0:T(8,128)S(1)}, s32[3,128,231]{1,2,0:T(8,128)}, u32[]{:S(2)}) copy-start(s32[3,128,231]{1,2,0:T(8,128)} %param.15) | copy-start | bytes 1064452
  203.2 20.7 %copy-start.6 = (f32[3,128,231]{1,2,0:T(8,128)}, f32[3,128,231]{1,2,0:T(8,128)S(1)}, u32[]{:S(2)}) copy-start(f32[3,128,231]{1,2,0:T(8,128)S(1)} %get-tuple-element.389) | copy-start | bytes 1064452
  223.7 6.8 %copy-start.9 = (f32[3,128,231]{1,0,2:T(4,128)}, f32[3,128,231]{1,0,2:T(4,128)S(1)}, u32[]{:S(2)}) copy-start(f32[3,128,231]{1,0,2:T(4,128)S(1)} %fusion.190) | copy-start | bytes 1064452
  232.7 16.1 %all-to-all-start.4 = ((bf16[822,16,32]{0,2,1:T(8,128)(2,1)}), bf16[822,16,32]{0,2,1:T(8,128)(2,1)S(1)}, u32[]{:S(2)}, u32[]{:S(2)}) async-start(bf16[822,16,32]{0,2,1:T(8,128)(2,1)} %bitcast.19), calls=%async_computation.4 | async-start | bytes 1835008 | tf_op jit(solution)/shard_map/all_to_all | solution.py:138
  251.8 3.8 copy-start.5
  259.0 13.4 %collective-permute-start.2 = (f32[6,137,192]{2,1,0:T(8,128)}, f32[6,137,192]{2,1,0:T(8,128)}, u32[]{:S(2)}, u32[]{:S(2)}) collective-permute-start(f32[6,137,192]{2,1,0:T(8,128)} %get-tuple-element.526), channel_id=1, source_target_pairs={{1,0},{2,1},{3,2},{4,3},{5,4},{6,5},{7,6},{8,7},{9,8},{10,9},{11,1... | collective-permute-start | bytes 1893896 | tf_op jit(solution)/shard_map/while/body/eval_jaxpr/ppermute | solution.py:24
  260.2 16.5 %collective-permute-start.3 = (f32[6,137,192]{2,1,0:T(8,128)S(1)}, f32[6,137,192]{2,1,0:T(8,128)}, u32[]{:S(2)}, u32[]{:S(2)}) collective-permute-start(f32[6,137,192]{2,1,0:T(8,128)S(1)} %get-tuple-element.527), channel_id=1, source_target_pairs={{0,1},{1,2},{2,3},{3,4},{4,5},{5,6},{6,7},{7,8},{8,9},{9,10},{10,1... | collective-permute-start | bytes 1893896 | tf_op jit(solution)/shard_map/while/body/eval_jaxpr/ppermute | solution.py:21
  290.4 2.4 copy-start
  294.8 1.2 copy-start.1
  299.3 13.4 %collective-permute-start.2 = (f32[6,137,192]{2,1,0:T(8,128)}, f32[6,137,192]{2,1,0:T(8,128)}, u32[]{:S(2)}, u32[]{:S(2)}) collective-permute-start(f32[6,137,192]{2,1,0:T(8,128)} %get-tuple-element.526), channel_id=1, source_target_pairs={{1,0},{2,1},{3,2},{4,3},{5,4},{6,5},{7,6},{8,7},{9,8},{10,9},{11,1... | collective-permute-start | bytes 1893896 | tf_op jit(solution)/shard_map/while/body/eval_jaxpr/ppermute | solution.py:24
  299.5 16.5 %collective-permute-start.3 = (f32[6,137,192]{2,1,0:T(8,128)S(1)}, f32[6,137,192]{2,1,0:T(8,128)}, u32[]{:S(2)}, u32[]{:S(2)}) collective-permute-start(f32[6,137,192]{2,1,0:T(8,128)S(1)} %get-tuple-element.527), channel_id=1, source_target_pairs={{0,1},{1,2},{2,3},{3,4},{4,5},{5,6},{6,7},{7,8},{8,9},{9,10},{10,1... | collective-permute-start | bytes 1893896 | tf_op jit(solution)/shard_map/while/body/eval_jaxpr/ppermute | solution.py:21
  329.6 2.4 copy-start
  334.1 1.2 copy-start.1
  337.3 0.8 copy-start.18
  340.7 1.9 copy-start.16
  398.3 0.8 copy-start.20
  405.1 1.0 copy-start.7
  405.1 1.1 copy-start.10
  405.1 1.2 copy-start.12
where the time goes:
time: 439 us; the launch traced here: 431 us
  blocking collectives  177 us (40%)
  waiting for transfers between devices  64.1 us (15%)
  local copies, waits for them, and re-layouts  61.2 us (14%)
  other arithmetic  60.9 us (14%)
  matrix products  41.2 us (9%)
  starting transfers between devices  19.9 us (5%)
  between operations  5.68 us (1%)
    psum x6, blocking collectives, by_axis(): value = lax.psum(value, axis)  53.8 us
    all_to_all x2, blocking collectives, sum_at_owner(): lax.all_to_all(pieces, axis, split_axis=0, concat_axis=0, tiled=True)  47.3 us
    add x20, other arithmetic, relax(): center + diffusion_rate * (north - center + (south - center) + west_ok *...  41.3 us
    ppermute x4, waiting for transfers between devices, with_halo(): lax.ppermute(lax.slice_in_dim(block, 0, width, axis=dim), axis, backward)  35.6 us
    all_to_all x2, blocking collectives, from_everyone(): lax.all_to_all(jnp.broadcast_to(value[None], (peers, *value.shape)), axis...  29.7 us
    all_gather x1, blocking collectives, gather_turned(): whole = lax.all_gather(both, axis, axis=0, tiled=True)  25.7 us
    all_to_all x2, blocking collectives, apply_operator(): lax.all_to_all(outbound, TILE, split_axis=1, concat_axis=1, tiled=True)  20.7 us
    ppermute x4, waiting for transfers between devices, with_halo(): lax.ppermute(lax.slice_in_dim(block, block.shape[dim] - width, None, axis...  16.1 us
  transfers between devices with their start and end apart: 10, of which 9 were waited for; matrix products, arithmetic and copies ran while one was open for 4% of the time, Pallas kernels for 0%

commit v1 on v0

--- a/solution.py
+++ b/solution.py
@@ -71,7 +71,7 @@
 
 def by_axis(value, axes):
     for axis in axes:
-        value = lax.psum(value, axis)
+        value = jnp.sum(lax.all_gather(value, axis), axis=0)
     return value
 
 

time: 439 us -> 460 us (1.048)
  blocking collectives: 177 us -> 133 us
  waiting for transfers between devices: 64.1 us -> 104 us
  starting transfers between devices: 19.9 us -> 33.5 us
  local copies, waits for them, and re-layouts: 61.2 us -> 70.7 us
    psum x6 -> x0, blocking collectives: 53.8 us -> none  [by_axis(): value = lax.psum(value, axis)]
    all_gather x0 -> x4, blocking collectives: none -> 42 us  [by_axis(): value = jnp.sum(lax.all_gather(value, axis), axis=0)]
    all_to_all x0 -> x3, waiting for transfers between devices: none -> 39.9 us  [the longest x2 24 us: from_everyone(): lax.all_to_all(jnp.broadcast_to(value[None], (peers, *value.shape)), axis...]
    all_to_all x2 -> x0, blocking collectives: 29.7 us -> none  [from_everyone(): lax.all_to_all(jnp.broadcast_to(value[None], (peers, *value.shape)), axis...]
    all_to_all x2 -> x1, blocking collectives: 47.3 us -> 26.8 us  [sum_at_owner(): lax.all_to_all(pieces, axis, split_axis=0, concat_axis=0, tiled=True)]
    unnamed x0 -> x2, blocking collectives: none -> 17.5 us
    all_to_all x0 -> x3, starting transfers between devices: none -> 11.7 us  [the longest x2 7.04 us: from_everyone(): lax.all_to_all(jnp.broadcast_to(value[None], (peers, *value.shape)), axis...]
    unnamed x40 -> x54, local copies, waits for them, and re-layouts: 15 us -> 21.7 us
  transfers between devices with their start and end apart: 10 -> 13, of which waited for: 9 -> 12; matrix products, arithmetic and copies ran while one was open for 4% -> 4% of each run, Pallas kernels for 0% -> 0%
where the time goes in v1:
time: 460 us; the launch traced here: 452 us
  blocking collectives  133 us (29%)
  waiting for transfers between devices  104 us (23%)
  local copies, waits for them, and re-layouts  70.7 us (15%)
  other arithmetic  63.5 us (14%)
  matrix products  41.1 us (9%)
  starting transfers between devices  33.5 us (7%)
  between operations  5.75 us (1%)
    all_gather x4, blocking collectives, by_axis(): value = jnp.sum(lax.all_gather(value, axis), axis=0)  42 us
    add x20, other arithmetic, relax(): center + diffusion_rate * (north - center + (south - center) + west_ok *...  41.3 us
    ppermute x4, waiting for transfers between devices, with_halo(): lax.ppermute(lax.slice_in_dim(block, 0, width, axis=dim), axis, backward)  35.6 us
    all_to_all x1, blocking collectives, sum_at_owner(): lax.all_to_all(pieces, axis, split_axis=0, concat_axis=0, tiled=True)  26.8 us
    all_gather x1, blocking collectives, gather_turned(): whole = lax.all_gather(both, axis, axis=0, tiled=True)  25.7 us
    all_to_all x2, waiting for transfers between devices, from_everyone(): lax.all_to_all(jnp.broadcast_to(value[None], (peers, *value.shape)), axis...  24 us
    unnamed x54, local copies, waits for them, and re-layouts  21.7 us
    all_to_all x2, blocking collectives, apply_operator(): lax.all_to_all(outbound, TILE, split_axis=1, concat_axis=1, tiled=True)  20.7 us
  transfers between devices with their start and end apart: 13, of which 12 were waited for; matrix products, arithmetic and copies ran while one was open for 4% of the time, Pallas kernels for 0%

profile of v1, /device:TPU:0, one launch (start us, length us, event | category | flops | bytes accessed | tf_op | source)
XLA Modules:
  0.0 452.2 jit_solution(10291996706908958864)
XLA Ops:
  0.6 13.2 %copy.93 = bf16[128,231,137]{1,2,0:T(8,128)(2,1)} copy(bf16[128,231,137]{0,1,2:T(8,128)(2,1)} %param.13) | data formatting | bytes 16203264 | tf_op args[2]
  14.1 6.2 %fusion.179 = bf16[3,137,128]{1,0,2:T(4,128)(2,1)S(1)} fusion(bf16[3,128,231]{2,0,1:T(4,128)(2,1)S(1)} %copy.92, bf16[128,231,137]{1,2,0:T(8,128)(2,1)} %copy.93), kind=kOutput, calls=%fused_computation.270 | convolution fusion | flops 24357504 | bytes 8384256 | tf_op jit(solution)/shard_map/ocl,poc->plo/dot_general | solution.py:129
  22.0 8.2 %all-to-all-start = ((bf16[411,16,32]{0,2,1:T(8,128)(2,1)}), bf16[411,16,32]{0,2,1:T(8,128)(2,1)S(1)}, u32[]{:S(2)}, u32[]{:S(2)}) async-start(bf16[411,16,32]{0,2,1:T(8,128)(2,1)} %bitcast.5), calls=%async_computation | async-start | bytes 1048576 | tf_op jit(solution)/shard_map/all_to_all | solution.py:138
  30.2 25.7 %all_gather.51 = s32[2048,2]{0,1:T(2,128)S(1)} all-gather(s32[128,2]{0,1:T(2,128)S(1)} %pad_add_fusion), channel_id=1, replica_groups=mesh['mem'=8,'tile_0'=4,'tile_1'=4] {'tile_0','tile_1'}, dimensions={0}, use_global_device_ids=true | all-gather | bytes 17408 | tf_op jit(solution)/shard_map/all_gather | solution.py:33
  56.0 8.0 %scatter_custom_fusion = s32[512]{0:T(512)S(1)} fusion(s32[2048]{0:T(1024)S(1)} %bitcast.122, s32[2048]{0:T(1024)S(1)} %add_select_fusion.12, s32[]{:T(128)} %constant.386.clone.1), kind=kCustom, calls=%fused_computation.340 | custom fusion | bytes 2052 | tf_op jit(solution)/shard_map/scatter | solution.py:117
  64.2 9.1 %scatter_custom_fusion.1 = pred[512]{0:T(512)(128)(4,1)S(1)} fusion(s32[2048]{0:T(1024)S(1)} %bitcast.123, pred[2048]{0:T(1024)(128)(4,1)S(1)} %broadcast.1456, pred[]{:T(512)} %constant.400.clone.1), kind=kCustom, calls=%fused_computation.342 | custom fusion | bytes 513 | tf_op jit(solution)/shard_map/scatter | solution.py:119
  75.0 1.9 fusion.183
  76.9 48.9 %while.32 = (s32[]{:T(128)}, f32[3,137,512]{2,1,0:T(8,128)S(1)}, bf16[2,137,512]{2,1,0:T(8,128)(2,1)S(1)}, f32[3,137,512]{2,1,0:T(8,128)S(1)}, bf16[137,137]{1,0:T(8,128)(2,1)S(1)}, /*index=5*/s32[]{:T(128)}, s32[]{:T(128)}) while((s32[]{:T(128)}, f32[3,137,512]{2,1,0:T(8,128)S(1)}, bf16[2,137,512]{2,1,0:T(8,128)(2,1)S(1)}, ...), condition=%wide.region_3.4_spmd.clone, body=%wide.region_2.3_spmd.clone.sunk | while | flops 77786176 | bytes 52359552 | solution.py:151
  78.8 2.1 collective-permute-start
  80.9 6.5 %collective-permute-done = f32[3,137,192]{2,1,0:T(8,128)} collective-permute-done((f32[3,137,192]{2,1,0:T(8,128)}, f32[3,137,192]{2,1,0:T(8,128)}, u32[]{:S(2)}, u32[]{:S(2)}) %collective-permute-start) | collective-permute-done | bytes 315680 | tf_op jit(solution)/shard_map/while/body/eval_jaxpr/ppermute | solution.py:24
  87.4 5.2 %collective-permute-done.1 = f32[3,137,192]{2,1,0:T(8,128)} collective-permute-done((f32[3,137,192]{2,1,0:T(8,128)S(1)}, f32[3,137,192]{2,1,0:T(8,128)}, u32[]{:S(2)}, u32[]{:S(2)}) %collective-permute-start.1) | collective-permute-done | bytes 315680 | tf_op jit(solution)/shard_map/while/body/eval_jaxpr/ppermute | solution.py:21
  94.2 1.7 fusion.266
  104.4 1.8 collective-permute-start.1
  106.3 6.5 %collective-permute-done = f32[3,137,192]{2,1,0:T(8,128)} collective-permute-done((f32[3,137,192]{2,1,0:T(8,128)}, f32[3,137,192]{2,1,0:T(8,128)}, u32[]{:S(2)}, u32[]{:S(2)}) %collective-permute-start) | collective-permute-done | bytes 315680 | tf_op jit(solution)/shard_map/while/body/eval_jaxpr/ppermute | solution.py:24
  112.8 3.3 collective-permute-done.1
  130.4 4.7 %all-to-all-start.1 = ((f32[8,411,16,4]{1,3,2,0:T(4,128)}), f32[8,411,16,4]{1,3,2,0:T(4,128)S(1)}, u32[]{:S(2)}, u32[]{:S(2)}) async-start(f32[8,411,16,4]{1,3,2,0:T(4,128)} %copy.99), calls=%async_computation.1 | async-start | bytes 2097152 | tf_op jit(solution)/shard_map/all_to_all | solution.py:50
  135.1 15.9 %all-to-all-done.1 = f32[8,411,16,4]{1,3,2,0:T(4,128)S(1)} async-done(((f32[8,411,16,4]{1,3,2,0:T(4,128)}), f32[8,411,16,4]{1,3,2,0:T(4,128)S(1)}, u32[]{:S(2)}, u32[]{:S(2)}) %all-to-all-start.1) | async-done | bytes 841760 | tf_op jit(solution)/shard_map/all_to_all | solution.py:50
  151.3 10.2 %all_to_all.48 = bf16[411,16,4]{0,2,1:T(4,128)(2,1)S(1)} all-to-all(bf16[411,16,4]{0,2,1:T(4,128)(2,1)S(1)} %multiply_convert_fusion.5), channel_id=1, replica_groups=mesh['mem'=8,'tile_0'=4,'tile_1'=4] {'tile_0','tile_1'}, dimensions={1} | all-to-all | bytes 105216 | tf_op jit(solution)/shard_map/all_to_all | solution.py:159
  162.4 3.5 all-to-all-start.3
  166.0 10.2 %all-to-all-done.3 = bf16[8,411,16,4]{1,3,2,0:T(4,128)(2,1)S(1)} async-done(((bf16[8,411,16,4]{1,3,2,0:T(4,128)(2,1)}), bf16[8,411,16,4]{1,3,2,0:T(4,128)(2,1)S(1)}, u32[]{:S(2)}, u32[]{:S(2)}) %all-to-all-start.3) | async-done | bytes 420896 | tf_op jit(solution)/shard_map/all_to_all | solution.py:56
  177.3 5.0 %convolution_bitcast_fusion.2 = f32[3,128,231]{2,0,1:T(4,128)S(1)} fusion(bf16[3,137,128]{1,0,2:T(4,128)(2,1)S(1)} %copy.101, bf16[128,231,137]{1,2,0:T(8,128)(2,1)} %copy.93), kind=kOutput, calls=%fused_computation.267 | convolution fusion | flops 24304896 | bytes 8561664 | tf_op jit(solution)/shard_map/ocl,plo->poc/dot_general | solution.py:166
  182.3 2.3 convolution_bitcast_fusion.5
  184.9 10.4 %all-gather.4 = f32[4,3,3]{2,1,0:T(4,128)S(1)} all-gather(f32[1,3,3]{2,1,0:T(4,128)S(1)} %convolution_bitcast_fusion.5), channel_id=2, replica_groups=mesh['mem'=8,'tile_0'=4,'tile_1'=4] {'tile_0'}, dimensions={0}, use_global_device_ids=true | all-gather | bytes 180 | tf_op jit(solution)/shard_map/all_gather | solution.py:74
  195.4 10.4 %all-gather.5 = f32[4,3,3]{2,1,0:T(4,128)S(1)} all-gather(f32[1,3,3]{2,1,0:T(4,128)S(1)} %bitcast.120), channel_id=3, replica_groups=mesh['mem'=8,'tile_0'=4,'tile_1'=4] {'tile_1'}, dimensions={0}, use_global_device_ids=true | all-gather | bytes 180 | tf_op jit(solution)/shard_map/all_gather | solution.py:74
  209.0 2.2 convolution_bitcast_fusion.3
  211.2 10.6 %all-gather.6 = f32[4,3,3]{2,1,0:T(4,128)S(1)} all-gather(f32[1,3,3]{2,1,0:T(4,128)S(1)} %convolution_bitcast_fusion.3), channel_id=4, replica_groups=mesh['mem'=8,'tile_0'=4,'tile_1'=4] {'tile_0'}, dimensions={0}, use_global_device_ids=true | all-gather | bytes 180 | tf_op jit(solution)/shard_map/all_gather | solution.py:74
  221.8 10.6 %all-gather.7 = f32[4,3,3]{2,1,0:T(4,128)S(1)} all-gather(f32[1,3,3]{2,1,0:T(4,128)S(1)} %bitcast.121), channel_id=5, replica_groups=mesh['mem'=8,'tile_0'=4,'tile_1'=4] {'tile_1'}, dimensions={0}, use_global_device_ids=true | all-gather | bytes 180 | tf_op jit(solution)/shard_map/all_gather | solution.py:74
  234.1 6.2 %fusion.178 = bf16[6,137,128]{1,0,2:T(8,128)(2,1)S(1)} fusion(bf16[6,128,231]{2,0,1:T(8,128)(2,1)S(1)} %copy.112, bf16[128,231,137]{1,2,0:T(8,128)(2,1)} %copy.93), kind=kOutput, calls=%fused_computation.266 | convolution fusion | flops 48715008 | bytes 8666880 | tf_op jit(solution)/shard_map/ocl,poc->plo/dot_general | solution.py:129
  242.5 5.4 %all-to-all-start.4 = ((bf16[822,16,32]{0,2,1:T(8,128)(2,1)}), bf16[822,16,32]{0,2,1:T(8,128)(2,1)S(1)}, u32[]{:S(2)}, u32[]{:S(2)}) async-start(bf16[822,16,32]{0,2,1:T(8,128)(2,1)} %bitcast.23), calls=%async_computation.4 | async-start | bytes 1835008 | tf_op jit(solution)/shard_map/all_to_all | solution.py:138
  247.9 12.5 %all-to-all-done.4 = bf16[822,16,32]{0,2,1:T(8,128)(2,1)S(1)} async-done(((bf16[822,16,32]{0,2,1:T(8,128)(2,1)}), bf16[822,16,32]{0,2,1:T(8,128)(2,1)S(1)}, u32[]{:S(2)}, u32[]{:S(2)}) %all-to-all-start.4) | async-done | bytes 841760 | tf_op jit(solution)/shard_map/all_to_all | solution.py:138
  260.4 3.0 dot_general.78
  263.4 3.9 fusion.176
  267.3 79.9 %while.33 = (s32[]{:T(128)}, f32[6,137,512]{2,1,0:T(8,128)}, bf16[2,137,512]{2,1,0:T(8,128)(2,1)S(1)}, f32[6,137,512]{2,1,0:T(8,128)}, bf16[137,137]{1,0:T(8,128)(2,1)S(1)}, /*index=5*/s32[]{:T(128)}, s32[]{:T(128)}) while((s32[]{:T(128)}, f32[6,137,512]{2,1,0:T(8,128)}, bf16[2,137,512]{2,1,0:T(8,128)(2,1)S(1)}, ...), condition=%wide.region_12.13_spmd.clone, body=%wide.region_11.12_spmd.clone.sunk | while | flops 155461888 | bytes 112613240 | solution.py:151
  267.5 2.0 convolution_bitcast_fusion.9
  272.7 11.3 %collective-permute-done.2 = f32[6,137,192]{2,1,0:T(8,128)} collective-permute-done((f32[6,137,192]{2,1,0:T(8,128)}, f32[6,137,192]{2,1,0:T(8,128)}, u32[]{:S(2)}, u32[]{:S(2)}) %collective-permute-start.2) | collective-permute-done | bytes 631328 | tf_op jit(solution)/shard_map/while/body/eval_jaxpr/ppermute | solution.py:24
  284.0 4.3 collective-permute-done.3
  288.3 2.3 pad_maximum_fusion.6
  290.6 3.4 fusion.280
  294.0 2.8 fusion.282
  296.8 2.8 fusion.284
  299.6 2.3 fusion.286
  302.0 2.3 fusion.288
  304.4 2.1 fusion.290
  307.7 2.0 convolution_bitcast_fusion.9
  311.1 1.8 collective-permute-start.3
  313.0 11.3 %collective-permute-done.2 = f32[6,137,192]{2,1,0:T(8,128)} collective-permute-done((f32[6,137,192]{2,1,0:T(8,128)}, f32[6,137,192]{2,1,0:T(8,128)}, u32[]{:S(2)}, u32[]{:S(2)}) %collective-permute-start.2) | collective-permute-done | bytes 631328 | tf_op jit(solution)/shard_map/while/body/eval_jaxpr/ppermute | solution.py:24
  324.3 3.3 collective-permute-done.3
  327.6 2.3 pad_maximum_fusion.6
  329.9 3.4 fusion.280
  333.3 2.8 fusion.282
  336.1 2.8 fusion.284
  338.9 2.3 fusion.286
  341.3 2.3 fusion.288
  343.6 2.1 fusion.290
  347.2 1.8 reshape.300
  349.7 2.7 gather_fusion.1
  352.4 1.8 gather.15
  355.0 26.8 %all_to_all.50 = f32[8,822,16,4]{1,3,2,0:T(4,128)S(1)} all-to-all(f32[8,822,16,4]{1,3,2,0:T(4,128)S(1)} %copy.119), channel_id=1, replica_groups=mesh['mem'=8,'tile_0'=4,'tile_1'=4] {'mem'}, dimensions={0} | all-to-all | bytes 3366912 | tf_op jit(solution)/shard_map/all_to_all | solution.py:50
  382.3 10.5 %all_to_all.49 = bf16[822,16,4]{0,2,1:T(4,128)(2,1)S(1)} all-to-all(bf16[822,16,4]{0,2,1:T(4,128)(2,1)S(1)} %multiply_convert_fusion.4), channel_id=1, replica_groups=mesh['mem'=8,'tile_0'=4,'tile_1'=4] {'tile_0','tile_1'}, dimensions={1} | all-to-all | bytes 210432 | tf_op jit(solution)/shard_map/all_to_all | solution.py:159
  394.0 3.6 all-to-all-start.7
  398.2 13.8 %all-to-all-done.7 = bf16[8,822,16,4]{1,3,2,0:T(4,128)(2,1)S(1)} async-done(((bf16[8,822,16,4]{1,3,2,0:T(4,128)(2,1)}), bf16[8,822,16,4]{1,3,2,0:T(4,128)(2,1)S(1)}, u32[]{:S(2)}, u32[]{:S(2)}) %all-to-all-start.7) | async-done | bytes 841760 | tf_op jit(solution)/shard_map/all_to_all | solution.py:56
  413.7 5.0 %fusion.218 = f32[128,6,231]{2,1,0:T(8,128)S(1)} fusion(bf16[6,137,128]{1,0,2:T(8,128)(2,1)S(1)} %copy.121, bf16[128,231,137]{1,2,0:T(8,128)(2,1)} %copy.93), kind=kOutput, calls=%fused_computation.351 | convolution fusion | flops 48609792 | bytes 9021696 | tf_op jit(solution)/shard_map/ocl,plo->poc/dot_general | solution.py:166
  424.9 8.6 %all-reduce.5 = (f32[4]{0:T(128)S(1)}, f32[4]{0:T(128)S(1)}) all-reduce(f32[4]{0:T(128)S(1)} %dynamic-update-slice.3, f32[4]{0:T(128)S(1)} %dynamic-update-slice.5), channel_id=1, replica_groups=mesh['mem'=8,'tile_0'=4,'tile_1'=4] {'tile_0'}, use_global_device_ids=true, to_apply=%add | all-reduce | flops 8 | bytes 64
  437.6 8.9 %all-reduce.4 = (f32[4]{0:T(128)S(1)}, f32[4]{0:T(128)S(1)}) all-reduce(f32[4]{0:T(128)S(1)} %dynamic-update-slice.4, f32[4]{0:T(128)S(1)} %dynamic-update-slice.6), channel_id=1, replica_groups=mesh['mem'=8,'tile_0'=4,'tile_1'=4] {'tile_1'}, use_global_device_ids=true, to_apply=%add.1 | all-reduce | flops 8 | bytes 64
  (193 shorter events, 63.6 us)
Async XLA Ops:
  0.6 13.2 %copy-start.13 = (s32[3,128,231]{1,2,0:T(8,128)S(1)}, s32[3,128,231]{1,2,0:T(8,128)}, u32[]{:S(2)}) copy-start(s32[3,128,231]{1,2,0:T(8,128)} %param.14) | copy-start | bytes 1064452
  14.1 6.4 %copy-start.21 = (s32[128]{0:T(128)S(1)}, s32[128]{0:T(128)}, u32[]{:S(2)}) copy-start(s32[128]{0:T(128)} %param.17) | copy-start | bytes 1540
  14.1 6.4 %copy-start.22 = (s32[128]{0:T(128)S(1)}, s32[128]{0:T(128)}, u32[]{:S(2)}) copy-start(s32[128]{0:T(128)} %param.16) | copy-start | bytes 1540
  20.4 43.7 %copy-start.14 = (bf16[2,137,512]{2,0,1:T(2,128)(2,1)S(1)}, bf16[2,137,512]{2,0,1:T(2,128)(2,1)}, u32[]{:S(2)}) copy-start(bf16[2,137,512]{2,0,1:T(2,128)(2,1)} %param.11) | copy-start | bytes 841732
  20.6 220.1 %copy-start.19 = (s32[128]{0:T(128)}, s32[128]{0:T(128)S(1)}, u32[]{:S(2)}) copy-start(s32[128]{0:T(128)S(1)} %multiply_add_fusion) | copy-start | bytes 1540
  22.0 51.5 %all-to-all-start = ((bf16[411,16,32]{0,2,1:T(8,128)(2,1)}), bf16[411,16,32]{0,2,1:T(8,128)(2,1)S(1)}, u32[]{:S(2)}, u32[]{:S(2)}) async-start(bf16[411,16,32]{0,2,1:T(8,128)(2,1)} %bitcast.5), calls=%async_computation | async-start | bytes 1048576 | tf_op jit(solution)/shard_map/all_to_all | solution.py:138
  64.2 64.8 %copy-start.15 = (pred[16,8,4]{2,1,0:T(8,128)(4,1)}, pred[16,8,4]{2,1,0:T(8,128)(4,1)S(1)}, u32[]{:S(2)}) copy-start(pred[16,8,4]{2,1,0:T(8,128)(4,1)S(1)} %broadcast_in_dim.137) | copy-start | bytes 1540
  73.4 53.6 %copy-start.17 = (s32[1024]{0:T(1024)}, s32[1024]{0:T(1024)S(1)}, u32[]{:S(2)}) copy-start(s32[1024]{0:T(1024)S(1)} %pad_clamp_fusion) | copy-start | bytes 12292
  73.4 3.5 copy-start.8
  76.9 0.7 copy-start.2
  78.8 8.6 %collective-permute-start = (f32[3,137,192]{2,1,0:T(8,128)}, f32[3,137,192]{2,1,0:T(8,128)}, u32[]{:S(2)}, u32[]{:S(2)}) collective-permute-start(f32[3,137,192]{2,1,0:T(8,128)} %get-tuple-element.507), channel_id=1, source_target_pairs={{1,0},{2,1},{3,2},{4,3},{5,4},{6,5},{7,6},{8,7},{9,8},{10,9},{11,1... | collective-permute-start | bytes 946952 | tf_op jit(solution)/shard_map/while/body/eval_jaxpr/ppermute | solution.py:24
  80.9 11.7 %collective-permute-start.1 = (f32[3,137,192]{2,1,0:T(8,128)S(1)}, f32[3,137,192]{2,1,0:T(8,128)}, u32[]{:S(2)}, u32[]{:S(2)}) collective-permute-start(f32[3,137,192]{2,1,0:T(8,128)S(1)} %get-tuple-element.508), channel_id=1, source_target_pairs={{0,1},{1,2},{2,3},{3,4},{4,5},{5,6},{6,7},{7,8},{8,9},{9,10},{10,1... | collective-permute-start | bytes 946952 | tf_op jit(solution)/shard_map/while/body/eval_jaxpr/ppermute | solution.py:21
  101.2 1.1 copy-start.3
  102.3 0.7 copy-start.2
  104.2 8.6 %collective-permute-start = (f32[3,137,192]{2,1,0:T(8,128)}, f32[3,137,192]{2,1,0:T(8,128)}, u32[]{:S(2)}, u32[]{:S(2)}) collective-permute-start(f32[3,137,192]{2,1,0:T(8,128)} %get-tuple-element.507), channel_id=1, source_target_pairs={{1,0},{2,1},{3,2},{4,3},{5,4},{6,5},{7,6},{8,7},{9,8},{10,9},{11,1... | collective-permute-start | bytes 946952 | tf_op jit(solution)/shard_map/while/body/eval_jaxpr/ppermute | solution.py:24
  104.4 11.7 %collective-permute-start.1 = (f32[3,137,192]{2,1,0:T(8,128)S(1)}, f32[3,137,192]{2,1,0:T(8,128)}, u32[]{:S(2)}, u32[]{:S(2)}) collective-permute-start(f32[3,137,192]{2,1,0:T(8,128)S(1)} %get-tuple-element.508), channel_id=1, source_target_pairs={{0,1},{1,2},{2,3},{3,4},{4,5},{5,6},{6,7},{7,8},{8,9},{9,10},{10,1... | collective-permute-start | bytes 946952 | tf_op jit(solution)/shard_map/while/body/eval_jaxpr/ppermute | solution.py:21
  124.7 1.1 copy-start.3
  125.8 0.7 copy-start.4
  130.4 20.6 %all-to-all-start.1 = ((f32[8,411,16,4]{1,3,2,0:T(4,128)}), f32[8,411,16,4]{1,3,2,0:T(4,128)S(1)}, u32[]{:S(2)}, u32[]{:S(2)}) async-start(f32[8,411,16,4]{1,3,2,0:T(4,128)} %copy.99), calls=%async_computation.1 | async-start | bytes 2097152 | tf_op jit(solution)/shard_map/all_to_all | solution.py:50
  135.1 30.9 %copy-start.11 = (s32[3,128,231]{1,2,0:T(8,128)S(1)}, s32[3,128,231]{1,2,0:T(8,128)}, u32[]{:S(2)}) copy-start(s32[3,128,231]{1,2,0:T(8,128)} %param.15) | copy-start | bytes 1064452
  162.4 13.7 %all-to-all-start.3 = ((bf16[8,411,16,4]{1,3,2,0:T(4,128)(2,1)}), bf16[8,411,16,4]{1,3,2,0:T(4,128)(2,1)S(1)}, u32[]{:S(2)}, u32[]{:S(2)}) async-start(bf16[8,411,16,4]{1,3,2,0:T(4,128)(2,1)} %broadcast_in_dim.146), calls=%async_computation.3 | async-start | bytes 1048576 | tf_op jit(solution)/shard_map/all_to_all | solution.py:56
  209.0 24.7 %copy-start.6 = (f32[3,128,231]{1,2,0:T(8,128)}, f32[3,128,231]{1,2,0:T(8,128)S(1)}, u32[]{:S(2)}) copy-start(f32[3,128,231]{1,2,0:T(8,128)S(1)} %get-tuple-element.389) | copy-start | bytes 1064452
  233.5 6.8 %copy-start.9 = (f32[3,128,231]{1,0,2:T(4,128)}, f32[3,128,231]{1,0,2:T(4,128)S(1)}, u32[]{:S(2)}) copy-start(f32[3,128,231]{1,0,2:T(4,128)S(1)} %fusion.190) | copy-start | bytes 1064452
  242.5 17.9 %all-to-all-start.4 = ((bf16[822,16,32]{0,2,1:T(8,128)(2,1)}), bf16[822,16,32]{0,2,1:T(8,128)(2,1)S(1)}, u32[]{:S(2)}, u32[]{:S(2)}) async-start(bf16[822,16,32]{0,2,1:T(8,128)(2,1)} %bitcast.23), calls=%async_computation.4 | async-start | bytes 1835008 | tf_op jit(solution)/shard_map/all_to_all | solution.py:138
  263.4 3.9 copy-start.5
  270.7 13.4 %collective-permute-start.2 = (f32[6,137,192]{2,1,0:T(8,128)}, f32[6,137,192]{2,1,0:T(8,128)}, u32[]{:S(2)}, u32[]{:S(2)}) collective-permute-start(f32[6,137,192]{2,1,0:T(8,128)} %get-tuple-element.526), channel_id=1, source_target_pairs={{1,0},{2,1},{3,2},{4,3},{5,4},{6,5},{7,6},{8,7},{9,8},{10,9},{11,1... | collective-permute-start | bytes 1893896 | tf_op jit(solution)/shard_map/while/body/eval_jaxpr/ppermute | solution.py:24
  271.9 16.5 %collective-permute-start.3 = (f32[6,137,192]{2,1,0:T(8,128)S(1)}, f32[6,137,192]{2,1,0:T(8,128)}, u32[]{:S(2)}, u32[]{:S(2)}) collective-permute-start(f32[6,137,192]{2,1,0:T(8,128)S(1)} %get-tuple-element.527), channel_id=1, source_target_pairs={{0,1},{1,2},{2,3},{3,4},{4,5},{5,6},{6,7},{7,8},{8,9},{9,10},{10,1... | collective-permute-start | bytes 1893896 | tf_op jit(solution)/shard_map/while/body/eval_jaxpr/ppermute | solution.py:21
  302.0 2.4 copy-start
  306.5 1.2 copy-start.1
  310.9 13.4 %collective-permute-start.2 = (f32[6,137,192]{2,1,0:T(8,128)}, f32[6,137,192]{2,1,0:T(8,128)}, u32[]{:S(2)}, u32[]{:S(2)}) collective-permute-start(f32[6,137,192]{2,1,0:T(8,128)} %get-tuple-element.526), channel_id=1, source_target_pairs={{1,0},{2,1},{3,2},{4,3},{5,4},{6,5},{7,6},{8,7},{9,8},{10,9},{11,1... | collective-permute-start | bytes 1893896 | tf_op jit(solution)/shard_map/while/body/eval_jaxpr/ppermute | solution.py:24
  311.1 16.5 %collective-permute-start.3 = (f32[6,137,192]{2,1,0:T(8,128)S(1)}, f32[6,137,192]{2,1,0:T(8,128)}, u32[]{:S(2)}, u32[]{:S(2)}) collective-permute-start(f32[6,137,192]{2,1,0:T(8,128)S(1)} %get-tuple-element.527), channel_id=1, source_target_pairs={{0,1},{1,2},{2,3},{3,4},{4,5},{5,6},{6,7},{7,8},{8,9},{9,10},{10,1... | collective-permute-start | bytes 1893896 | tf_op jit(solution)/shard_map/while/body/eval_jaxpr/ppermute | solution.py:21
  341.3 2.4 copy-start
  345.8 1.2 copy-start.1
  348.9 0.8 copy-start.18
  352.4 1.9 copy-start.16
  382.2 15.3 %copy-start.24 = (u32[128]{0:T(128)S(1)}, u32[128]{0:T(128)}, u32[]{:S(2)}) copy-start(u32[128]{0:T(128)} %constant.412) | copy-start | bytes 1540
  394.0 18.0 %all-to-all-start.7 = ((bf16[8,822,16,4]{1,3,2,0:T(4,128)(2,1)}), bf16[8,822,16,4]{1,3,2,0:T(4,128)(2,1)S(1)}, u32[]{:S(2)}, u32[]{:S(2)}) async-start(bf16[8,822,16,4]{1,3,2,0:T(4,128)(2,1)} %broadcast_in_dim.148), calls=%async_computation.7 | async-start | bytes 1835008 | tf_op jit(solution)/shard_map/all_to_all | solution.py:56
  412.0 0.8 copy-start.20
  418.7 1.0 copy-start.7
  418.8 1.1 copy-start.10
  418.8 1.2 copy-start.12
  418.8 5.6 %copy-start.23 = (u32[128]{0:T(128)S(1)}, u32[128]{0:T(128)}, u32[]{:S(2)}) copy-start(u32[128]{0:T(128)} %constant.417) | copy-start | bytes 1540
